TPU v7x, 32 devices: a whole 2x2x4 slice. The times are simulated.
32 devices in a mesh: row: 4 (over x, core), col: 8 (over z, y).
Axes of the slice: x: 2, y: 2, z: 4, core: 2. Of those that a mesh axis runs over, the one named last changes fastest.
Arguments:
- optical_field: float32 [2, 512, 4096], P(None, 'row', 'col'), may hold values from -6 to 6
- index_panels: bfloat16 [5, 512, 4096], P(None, ('row', 'col')), may hold values from -4 to 4
Outputs:
- propagated: float32 [2, 512, 4096], P(None, 'row', 'col')
All inputs are finite; a program needn't handle non-finite values.
Results may differ from a plain program's by a relative error of at most 0.0003.
Values may be sent and summed in bfloat16 or wider, within the bound.
A program may use at most 64 MiB of HBM per device.

v0:
```python
import jax
import jax.numpy as jnp
from jax import lax
from jax.sharding import PartitionSpec as P

STEPS = 2
diffraction = 0.15
phase_gain = 0.25


def with_halo(cells, sides, width):
    for axis, dim in sides:
        count = lax.axis_size(axis)
        head = lax.slice_in_dim(cells, 0, width, axis=dim)
        tail = lax.slice_in_dim(cells, cells.shape[dim] - width, cells.shape[dim], axis=dim)
        cells = jnp.concatenate(
            [
                lax.ppermute(tail, axis, [(i, (i + 1) % count) for i in range(count)]),
                cells,
                lax.ppermute(head, axis, [((i + 1) % count, i) for i in range(count)]),
            ],
            axis=dim,
        )
    return cells


def laplace(padded):
    centre = padded[:, 2:-2, 2:-2]
    along_y = 16.0 * (padded[:, 1:-3, 2:-2] + padded[:, 3:-1, 2:-2]) - (
        padded[:, :-4, 2:-2] + padded[:, 4:, 2:-2]
    )
    along_x = 16.0 * (padded[:, 2:-2, 1:-3] + padded[:, 2:-2, 3:-1]) - (
        padded[:, 2:-2, :-4] + padded[:, 2:-2, 4:]
    )
    return (along_y + along_x - 60.0 * centre) / 12.0


def slope(padded, plane):
    centre = padded[:, 2:-2, 2:-2]
    total = diffraction * laplace(padded) + phase_gain * plane.astype(jnp.float32) * centre
    return jnp.stack([-total[1], total[0]])


def section_slope(state, plane):
    padded = with_halo(state, (("row", 1), ("col", 2)), 2)
    return slope(padded, plane)


def local(optical_field, index_panels):
    planes_all = lax.all_to_all(index_panels, "col", split_axis=2, concat_axis=1, tiled=True)
    field = optical_field
    planes = None
    for step_index in range(STEPS):
        first = 2 * step_index
        planes = planes_all[first : first + 3]
        first_slope = section_slope(field, planes[0])
        second_slope = section_slope(field + 0.5 * first_slope, planes[1])
        third_slope = section_slope(field + 0.5 * second_slope, planes[1])
        fourth_slope = section_slope(field + third_slope, planes[2])
        field = field + (first_slope + 2.0 * second_slope + 2.0 * third_slope + fourth_slope) / 6.0
    return field


def solution(mesh):
    in_specs = (P(None, "row", "col"), P(None, ("row", "col"), None))
    out_specs = P(None, "row", "col")
    return jax.shard_map(local, mesh=mesh, in_specs=in_specs, out_specs=out_specs, check_vma=False)
```

profile of v0, /device:TPU:0, one launch (start us, length us, event | category | flops | bytes accessed | tf_op | source)
XLA Modules:
  0.0 162.4 jit_solution(11394870547222477419)
XLA Ops:
  0.0 8.1 %copy.10 = bf16[5,16,4096]{1,0,2:T(8,128)(2,1)} copy(bf16[5,16,4096]{2,1,0:T(8,128)(2,1)} %param.3) | data formatting | bytes 1310720 | tf_op args[1]
  8.1 9.1 %reshape.60 = bf16[8,2,20480]{2,1,0:T(2,128)(2,1)} reshape(bf16[4096,5,16]{2,1,0:T(8,128)(2,1)} %bitcast.10) | data formatting | bytes 1310720
  17.2 7.3 %all-to-all-start = ((bf16[8,2,20480]{2,1,0:T(2,128)(2,1)}), bf16[8,2,20480]{2,1,0:T(2,128)(2,1)S(1)}, u32[]{:S(2)}, u32[]{:S(2)}) async-start(bf16[8,2,20480]{2,1,0:T(2,128)(2,1)} %reshape.60), calls=%async_computation | async-start | bytes 1310720 | tf_op jit(solution)/shard_map/all_to_all | solution.py:50
  24.5 1.7 %collective-permute-start.1 = (f32[2,2,512]{2,1,0:T(2,128)S(1)}, f32[2,2,512]{2,1,0:T(2,128)S(1)}, u32[]{:S(2)}, u32[]{:S(2)}) collective-permute-start(f32[2,2,512]{2,1,0:T(2,128)S(1)} %get-tuple-element.72), channel_id=1, source_target_pairs={{8,0},{16,8},{24,16},{0,24},{9,1},{17,9},{25,17},{1,25},{10,2},{18... | collective-permute-start | bytes 24584 | tf_op jit(solution)/shard_map/ppermute | solution.py:20
  26.3 1.3 collective-permute-done
  27.8 2.1 %collective-permute-start.2 = (f32[2,132,2]{2,1,0:T(8,128)S(1)}, f32[2,132,2]{2,1,0:T(8,128)S(1)}, u32[]{:S(2)}, u32[]{:S(2)}) collective-permute-start(f32[2,132,2]{2,1,0:T(8,128)S(1)} %get-tuple-element.40), channel_id=1, source_target_pairs={{0,1},{1,2},{2,3},{3,4},{4,5},{5,6},{6,7},{7,0},{8,9},{9,10},{10,1... | collective-permute-start | bytes 6344 | tf_op jit(solution)/shard_map/ppermute | solution.py:18
  29.8 2.8 %collective-permute-start.3 = (f32[2,132,2]{2,1,0:T(8,128)S(1)}, f32[2,132,2]{2,1,0:T(8,128)S(1)}, u32[]{:S(2)}, u32[]{:S(2)}) collective-permute-start(f32[2,132,2]{2,1,0:T(8,128)S(1)} %get-tuple-element.41), channel_id=1, source_target_pairs={{1,0},{2,1},{3,2},{4,3},{5,4},{6,5},{7,6},{0,7},{9,8},{10,9},{11,1... | collective-permute-start | bytes 6344 | tf_op jit(solution)/shard_map/ppermute | solution.py:20
  32.6 10.5 %collective-permute-done.2 = f32[2,132,2]{2,1,0:T(8,128)S(1)} collective-permute-done((f32[2,132,2]{2,1,0:T(8,128)S(1)}, f32[2,132,2]{2,1,0:T(8,128)S(1)}, u32[]{:S(2)}, u32[]{:S(2)}) %collective-permute-start.2) | collective-permute-done | bytes 2144 | tf_op jit(solution)/shard_map/ppermute | solution.py:18
  43.4 7.3 %reshape.61 = bf16[4096,5,16]{2,1,0:T(8,128)(2,1)} reshape(bf16[8,2,20480]{2,1,0:T(2,128)(2,1)S(1)} %all-to-all-done) | data formatting | bytes 1310720
  50.7 6.4 %copy.17 = bf16[5,16,8,512]{3,2,1,0:T(8,128)(2,1)S(1)} copy(bf16[5,16,8,512]{1,0,3,2:T(8,128)(2,1)} %bitcast.9) | data formatting | bytes 1310720 | tf_op jit(solution)/shard_map/all_to_all | solution.py:50
  58.3 1.7 %collective-permute-start.5 = (f32[2,2,512]{2,1,0:T(2,128)S(1)}, f32[2,2,512]{2,1,0:T(2,128)S(1)}, u32[]{:S(2)}, u32[]{:S(2)}) collective-permute-start(f32[2,2,512]{2,1,0:T(2,128)S(1)} %get-tuple-element.69), channel_id=1, source_target_pairs={{8,0},{16,8},{24,16},{0,24},{9,1},{17,9},{25,17},{1,25},{10,2},{18... | collective-permute-start | bytes 24584 | tf_op jit(solution)/shard_map/ppermute | solution.py:20
  60.0 1.3 collective-permute-done.4
  61.5 2.8 %collective-permute-start.6 = (f32[2,132,2]{2,1,0:T(8,128)S(1)}, f32[2,132,2]{2,1,0:T(8,128)S(1)}, u32[]{:S(2)}, u32[]{:S(2)}) collective-permute-start(f32[2,132,2]{2,1,0:T(8,128)S(1)} %get-tuple-element.36), channel_id=1, source_target_pairs={{0,1},{1,2},{2,3},{3,4},{4,5},{5,6},{6,7},{7,0},{8,9},{9,10},{10,1... | collective-permute-start | bytes 6344 | tf_op jit(solution)/shard_map/ppermute | solution.py:18
  64.3 2.0 %collective-permute-start.7 = (f32[2,132,2]{2,1,0:T(8,128)S(1)}, f32[2,132,2]{2,1,0:T(8,128)S(1)}, u32[]{:S(2)}, u32[]{:S(2)}) collective-permute-start(f32[2,132,2]{2,1,0:T(8,128)S(1)} %get-tuple-element.37), channel_id=1, source_target_pairs={{1,0},{2,1},{3,2},{4,3},{5,4},{6,5},{7,6},{0,7},{9,8},{10,9},{11,1... | collective-permute-start | bytes 6344 | tf_op jit(solution)/shard_map/ppermute | solution.py:20
  66.5 4.4 %collective-permute-done.6 = f32[2,132,2]{2,1,0:T(8,128)S(1)} collective-permute-done((f32[2,132,2]{2,1,0:T(8,128)S(1)}, f32[2,132,2]{2,1,0:T(8,128)S(1)}, u32[]{:S(2)}, u32[]{:S(2)}) %collective-permute-start.6) | collective-permute-done | bytes 2144 | tf_op jit(solution)/shard_map/ppermute | solution.py:18
  70.8 2.9 %collective-permute-done.7 = f32[2,132,2]{2,1,0:T(8,128)S(1)} collective-permute-done((f32[2,132,2]{2,1,0:T(8,128)S(1)}, f32[2,132,2]{2,1,0:T(8,128)S(1)}, u32[]{:S(2)}, u32[]{:S(2)}) %collective-permute-start.7) | collective-permute-done | bytes 2144 | tf_op jit(solution)/shard_map/ppermute | solution.py:20
  74.1 0.6 fusion.61
  75.0 1.6 %collective-permute-start.9 = (f32[2,2,512]{2,1,0:T(2,128)S(1)}, f32[2,2,512]{2,1,0:T(2,128)S(1)}, u32[]{:S(2)}, u32[]{:S(2)}) collective-permute-start(f32[2,2,512]{2,1,0:T(2,128)S(1)} %get-tuple-element.65), channel_id=1, source_target_pairs={{8,0},{16,8},{24,16},{0,24},{9,1},{17,9},{25,17},{1,25},{10,2},{18... | collective-permute-start | bytes 24584 | tf_op jit(solution)/shard_map/ppermute | solution.py:20
  76.7 1.3 collective-permute-done.8
  78.2 4.7 %collective-permute-start.11 = (f32[2,132,2]{2,1,0:T(8,128)S(1)}, f32[2,132,2]{2,1,0:T(8,128)S(1)}, u32[]{:S(2)}, u32[]{:S(2)}) collective-permute-start(f32[2,132,2]{2,1,0:T(8,128)S(1)} %get-tuple-element.33), channel_id=1, source_target_pairs={{1,0},{2,1},{3,2},{4,3},{5,4},{6,5},{7,6},{0,7},{9,8},{10,9},{11,1... | collective-permute-start | bytes 6344 | tf_op jit(solution)/shard_map/ppermute | solution.py:20
  82.9 4.6 %collective-permute-done.10 = f32[2,132,2]{2,1,0:T(8,128)S(1)} collective-permute-done((f32[2,132,2]{2,1,0:T(8,128)S(1)}, f32[2,132,2]{2,1,0:T(8,128)S(1)}, u32[]{:S(2)}, u32[]{:S(2)}) %collective-permute-start.10) | collective-permute-done | bytes 2144 | tf_op jit(solution)/shard_map/ppermute | solution.py:18
  88.1 0.6 fusion.52
  89.0 1.6 %collective-permute-start.13 = (f32[2,2,512]{2,1,0:T(2,128)S(1)}, f32[2,2,512]{2,1,0:T(2,128)S(1)}, u32[]{:S(2)}, u32[]{:S(2)}) collective-permute-start(f32[2,2,512]{2,1,0:T(2,128)S(1)} %get-tuple-element.61), channel_id=1, source_target_pairs={{8,0},{16,8},{24,16},{0,24},{9,1},{17,9},{25,17},{1,25},{10,2},{18... | collective-permute-start | bytes 24584 | tf_op jit(solution)/shard_map/ppermute | solution.py:20
  90.6 1.3 collective-permute-done.12
  92.2 4.7 %collective-permute-start.15 = (f32[2,132,2]{2,1,0:T(8,128)S(1)}, f32[2,132,2]{2,1,0:T(8,128)S(1)}, u32[]{:S(2)}, u32[]{:S(2)}) collective-permute-start(f32[2,132,2]{2,1,0:T(8,128)S(1)} %get-tuple-element.29), channel_id=1, source_target_pairs={{1,0},{2,1},{3,2},{4,3},{5,4},{6,5},{7,6},{0,7},{9,8},{10,9},{11,1... | collective-permute-start | bytes 6344 | tf_op jit(solution)/shard_map/ppermute | solution.py:20
  97.1 4.2 %collective-permute-done.14 = f32[2,132,2]{2,1,0:T(8,128)S(1)} collective-permute-done((f32[2,132,2]{2,1,0:T(8,128)S(1)}, f32[2,132,2]{2,1,0:T(8,128)S(1)}, u32[]{:S(2)}, u32[]{:S(2)}) %collective-permute-start.14) | collective-permute-done | bytes 2144 | tf_op jit(solution)/shard_map/ppermute | solution.py:18
  101.5 0.6 fusion.43
  102.9 1.4 collective-permute-start.17
  104.3 1.3 collective-permute-done.16
  105.9 5.1 %collective-permute-start.19 = (f32[2,132,2]{2,1,0:T(8,128)S(1)}, f32[2,132,2]{2,1,0:T(8,128)S(1)}, u32[]{:S(2)}, u32[]{:S(2)}) collective-permute-start(f32[2,132,2]{2,1,0:T(8,128)S(1)} %get-tuple-element.25), channel_id=1, source_target_pairs={{1,0},{2,1},{3,2},{4,3},{5,4},{6,5},{7,6},{0,7},{9,8},{10,9},{11,1... | collective-permute-start | bytes 6344 | tf_op jit(solution)/shard_map/ppermute | solution.py:20
  111.0 3.8 %collective-permute-done.18 = f32[2,132,2]{2,1,0:T(8,128)S(1)} collective-permute-done((f32[2,132,2]{2,1,0:T(8,128)S(1)}, f32[2,132,2]{2,1,0:T(8,128)S(1)}, u32[]{:S(2)}, u32[]{:S(2)}) %collective-permute-start.18) | collective-permute-done | bytes 2144 | tf_op jit(solution)/shard_map/ppermute | solution.py:18
  116.9 1.3 collective-permute-start.21
  118.1 1.3 collective-permute-done.20
  119.7 5.3 %collective-permute-start.23 = (f32[2,132,2]{2,1,0:T(8,128)S(1)}, f32[2,132,2]{2,1,0:T(8,128)S(1)}, u32[]{:S(2)}, u32[]{:S(2)}) collective-permute-start(f32[2,132,2]{2,1,0:T(8,128)S(1)} %get-tuple-element.21), channel_id=1, source_target_pairs={{1,0},{2,1},{3,2},{4,3},{5,4},{6,5},{7,6},{0,7},{9,8},{10,9},{11,1... | collective-permute-start | bytes 6344 | tf_op jit(solution)/shard_map/ppermute | solution.py:20
  125.1 3.9 %collective-permute-done.22 = f32[2,132,2]{2,1,0:T(8,128)S(1)} collective-permute-done((f32[2,132,2]{2,1,0:T(8,128)S(1)}, f32[2,132,2]{2,1,0:T(8,128)S(1)}, u32[]{:S(2)}, u32[]{:S(2)}) %collective-permute-start.22) | collective-permute-done | bytes 2144 | tf_op jit(solution)/shard_map/ppermute | solution.py:18
  129.0 0.9 collective-permute-done.23
  130.2 0.6 fusion.25
  131.4 1.6 %collective-permute-start.25 = (f32[2,2,512]{2,1,0:T(2,128)S(1)}, f32[2,2,512]{2,1,0:T(2,128)S(1)}, u32[]{:S(2)}, u32[]{:S(2)}) collective-permute-start(f32[2,2,512]{2,1,0:T(2,128)S(1)} %get-tuple-element.49), channel_id=1, source_target_pairs={{8,0},{16,8},{24,16},{0,24},{9,1},{17,9},{25,17},{1,25},{10,2},{18... | collective-permute-start | bytes 24584 | tf_op jit(solution)/shard_map/ppermute | solution.py:20
  133.0 1.3 collective-permute-done.24
  134.7 4.5 %collective-permute-start.27 = (f32[2,132,2]{2,1,0:T(8,128)S(1)}, f32[2,132,2]{2,1,0:T(8,128)S(1)}, u32[]{:S(2)}, u32[]{:S(2)}) collective-permute-start(f32[2,132,2]{2,1,0:T(8,128)S(1)} %get-tuple-element.17), channel_id=1, source_target_pairs={{1,0},{2,1},{3,2},{4,3},{5,4},{6,5},{7,6},{0,7},{9,8},{10,9},{11,1... | collective-permute-start | bytes 6344 | tf_op jit(solution)/shard_map/ppermute | solution.py:20
  139.3 4.2 %collective-permute-done.26 = f32[2,132,2]{2,1,0:T(8,128)S(1)} collective-permute-done((f32[2,132,2]{2,1,0:T(8,128)S(1)}, f32[2,132,2]{2,1,0:T(8,128)S(1)}, u32[]{:S(2)}, u32[]{:S(2)}) %collective-permute-start.26) | collective-permute-done | bytes 2144 | tf_op jit(solution)/shard_map/ppermute | solution.py:18
  143.5 1.5 collective-permute-done.27
  146.5 1.6 %collective-permute-start.29 = (f32[2,2,512]{2,1,0:T(2,128)S(1)}, f32[2,2,512]{2,1,0:T(2,128)S(1)}, u32[]{:S(2)}, u32[]{:S(2)}) collective-permute-start(f32[2,2,512]{2,1,0:T(2,128)S(1)} %get-tuple-element.45), channel_id=1, source_target_pairs={{8,0},{16,8},{24,16},{0,24},{9,1},{17,9},{25,17},{1,25},{10,2},{18... | collective-permute-start | bytes 24584 | tf_op jit(solution)/shard_map/ppermute | solution.py:20
  148.1 1.3 collective-permute-done.28
  149.8 4.5 %collective-permute-start.31 = (f32[2,132,2]{2,1,0:T(8,128)S(1)}, f32[2,132,2]{2,1,0:T(8,128)S(1)}, u32[]{:S(2)}, u32[]{:S(2)}) collective-permute-start(f32[2,132,2]{2,1,0:T(8,128)S(1)} %get-tuple-element.13), channel_id=1, source_target_pairs={{1,0},{2,1},{3,2},{4,3},{5,4},{6,5},{7,6},{0,7},{9,8},{10,9},{11,1... | collective-permute-start | bytes 6344 | tf_op jit(solution)/shard_map/ppermute | solution.py:20
  154.5 4.0 %collective-permute-done.30 = f32[2,132,2]{2,1,0:T(8,128)S(1)} collective-permute-done((f32[2,132,2]{2,1,0:T(8,128)S(1)}, f32[2,132,2]{2,1,0:T(8,128)S(1)}, u32[]{:S(2)}, u32[]{:S(2)}) %collective-permute-start.30) | collective-permute-done | bytes 2144 | tf_op jit(solution)/shard_map/ppermute | solution.py:18
  158.6 1.5 collective-permute-done.31
  161.0 1.4 fusion.97
  (80 shorter events, 11.9 us)
Async XLA Ops:
  0.0 24.5 %copy-start = (f32[2,128,512]{2,1,0:T(8,128)S(1)}, f32[2,128,512]{2,1,0:T(8,128)}, u32[]{:S(2)}) copy-start(f32[2,128,512]{2,1,0:T(8,128)} %param.2) | copy-start | bytes 1572868
  17.2 26.2 %all-to-all-start = ((bf16[8,2,20480]{2,1,0:T(2,128)(2,1)}), bf16[8,2,20480]{2,1,0:T(2,128)(2,1)S(1)}, u32[]{:S(2)}, u32[]{:S(2)}) async-start(bf16[8,2,20480]{2,1,0:T(2,128)(2,1)} %reshape.60), calls=%async_computation | async-start | bytes 1310720 | tf_op jit(solution)/shard_map/all_to_all | solution.py:50
  24.5 3.1 %collective-permute-start = (f32[2,2,512]{2,1,0:T(2,128)S(1)}, f32[2,2,512]{2,1,0:T(2,128)S(1)}, u32[]{:S(2)}, u32[]{:S(2)}) collective-permute-start(f32[2,2,512]{2,1,0:T(2,128)S(1)} %get-tuple-element.73), channel_id=1, source_target_pairs={{0,8},{8,16},{16,24},{24,0},{1,9},{9,17},{17,25},{25,1},{2,10},{10... | collective-permute-start | bytes 24584 | tf_op jit(solution)/shard_map/ppermute | solution.py:18
  24.5 3.1 %collective-permute-start.1 = (f32[2,2,512]{2,1,0:T(2,128)S(1)}, f32[2,2,512]{2,1,0:T(2,128)S(1)}, u32[]{:S(2)}, u32[]{:S(2)}) collective-permute-start(f32[2,2,512]{2,1,0:T(2,128)S(1)} %get-tuple-element.72), channel_id=1, source_target_pairs={{8,0},{16,8},{24,16},{0,24},{9,1},{17,9},{25,17},{1,25},{10,2},{18... | collective-permute-start | bytes 24584 | tf_op jit(solution)/shard_map/ppermute | solution.py:20
  27.8 15.4 %collective-permute-start.2 = (f32[2,132,2]{2,1,0:T(8,128)S(1)}, f32[2,132,2]{2,1,0:T(8,128)S(1)}, u32[]{:S(2)}, u32[]{:S(2)}) collective-permute-start(f32[2,132,2]{2,1,0:T(8,128)S(1)} %get-tuple-element.40), channel_id=1, source_target_pairs={{0,1},{1,2},{2,3},{3,4},{4,5},{5,6},{6,7},{7,0},{8,9},{9,10},{10,1... | collective-permute-start | bytes 6344 | tf_op jit(solution)/shard_map/ppermute | solution.py:18
  29.8 13.3 %collective-permute-start.3 = (f32[2,132,2]{2,1,0:T(8,128)S(1)}, f32[2,132,2]{2,1,0:T(8,128)S(1)}, u32[]{:S(2)}, u32[]{:S(2)}) collective-permute-start(f32[2,132,2]{2,1,0:T(8,128)S(1)} %get-tuple-element.41), channel_id=1, source_target_pairs={{1,0},{2,1},{3,2},{4,3},{5,4},{6,5},{7,6},{0,7},{9,8},{10,9},{11,1... | collective-permute-start | bytes 6344 | tf_op jit(solution)/shard_map/ppermute | solution.py:20
  58.2 3.1 %collective-permute-start.4 = (f32[2,2,512]{2,1,0:T(2,128)S(1)}, f32[2,2,512]{2,1,0:T(2,128)S(1)}, u32[]{:S(2)}, u32[]{:S(2)}) collective-permute-start(f32[2,2,512]{2,1,0:T(2,128)S(1)} %get-tuple-element.68), channel_id=1, source_target_pairs={{0,8},{8,16},{16,24},{24,0},{1,9},{9,17},{17,25},{25,1},{2,10},{10... | collective-permute-start | bytes 24584 | tf_op jit(solution)/shard_map/ppermute | solution.py:18
  58.3 3.1 %collective-permute-start.5 = (f32[2,2,512]{2,1,0:T(2,128)S(1)}, f32[2,2,512]{2,1,0:T(2,128)S(1)}, u32[]{:S(2)}, u32[]{:S(2)}) collective-permute-start(f32[2,2,512]{2,1,0:T(2,128)S(1)} %get-tuple-element.69), channel_id=1, source_target_pairs={{8,0},{16,8},{24,16},{0,24},{9,1},{17,9},{25,17},{1,25},{10,2},{18... | collective-permute-start | bytes 24584 | tf_op jit(solution)/shard_map/ppermute | solution.py:20
  61.5 9.3 %collective-permute-start.6 = (f32[2,132,2]{2,1,0:T(8,128)S(1)}, f32[2,132,2]{2,1,0:T(8,128)S(1)}, u32[]{:S(2)}, u32[]{:S(2)}) collective-permute-start(f32[2,132,2]{2,1,0:T(8,128)S(1)} %get-tuple-element.36), channel_id=1, source_target_pairs={{0,1},{1,2},{2,3},{3,4},{4,5},{5,6},{6,7},{7,0},{8,9},{9,10},{10,1... | collective-permute-start | bytes 6344 | tf_op jit(solution)/shard_map/ppermute | solution.py:18
  64.3 9.4 %collective-permute-start.7 = (f32[2,132,2]{2,1,0:T(8,128)S(1)}, f32[2,132,2]{2,1,0:T(8,128)S(1)}, u32[]{:S(2)}, u32[]{:S(2)}) collective-permute-start(f32[2,132,2]{2,1,0:T(8,128)S(1)} %get-tuple-element.37), channel_id=1, source_target_pairs={{1,0},{2,1},{3,2},{4,3},{5,4},{6,5},{7,6},{0,7},{9,8},{10,9},{11,1... | collective-permute-start | bytes 6344 | tf_op jit(solution)/shard_map/ppermute | solution.py:20
  74.9 3.1 %collective-permute-start.8 = (f32[2,2,512]{2,1,0:T(2,128)S(1)}, f32[2,2,512]{2,1,0:T(2,128)S(1)}, u32[]{:S(2)}, u32[]{:S(2)}) collective-permute-start(f32[2,2,512]{2,1,0:T(2,128)S(1)} %get-tuple-element.64), channel_id=1, source_target_pairs={{0,8},{8,16},{16,24},{24,0},{1,9},{9,17},{17,25},{25,1},{2,10},{10... | collective-permute-start | bytes 24584 | tf_op jit(solution)/shard_map/ppermute | solution.py:18
  75.0 3.0 %collective-permute-start.9 = (f32[2,2,512]{2,1,0:T(2,128)S(1)}, f32[2,2,512]{2,1,0:T(2,128)S(1)}, u32[]{:S(2)}, u32[]{:S(2)}) collective-permute-start(f32[2,2,512]{2,1,0:T(2,128)S(1)} %get-tuple-element.65), channel_id=1, source_target_pairs={{8,0},{16,8},{24,16},{0,24},{9,1},{17,9},{25,17},{1,25},{10,2},{18... | collective-permute-start | bytes 24584 | tf_op jit(solution)/shard_map/ppermute | solution.py:20
  78.2 9.3 %collective-permute-start.10 = (f32[2,132,2]{2,1,0:T(8,128)S(1)}, f32[2,132,2]{2,1,0:T(8,128)S(1)}, u32[]{:S(2)}, u32[]{:S(2)}) collective-permute-start(f32[2,132,2]{2,1,0:T(8,128)S(1)} %get-tuple-element.32), channel_id=1, source_target_pairs={{0,1},{1,2},{2,3},{3,4},{4,5},{5,6},{6,7},{7,0},{8,9},{9,10},{10,1... | collective-permute-start | bytes 6344 | tf_op jit(solution)/shard_map/ppermute | solution.py:18
  78.2 9.5 %collective-permute-start.11 = (f32[2,132,2]{2,1,0:T(8,128)S(1)}, f32[2,132,2]{2,1,0:T(8,128)S(1)}, u32[]{:S(2)}, u32[]{:S(2)}) collective-permute-start(f32[2,132,2]{2,1,0:T(8,128)S(1)} %get-tuple-element.33), channel_id=1, source_target_pairs={{1,0},{2,1},{3,2},{4,3},{5,4},{6,5},{7,6},{0,7},{9,8},{10,9},{11,1... | collective-permute-start | bytes 6344 | tf_op jit(solution)/shard_map/ppermute | solution.py:20
  88.8 3.1 %collective-permute-start.12 = (f32[2,2,512]{2,1,0:T(2,128)S(1)}, f32[2,2,512]{2,1,0:T(2,128)S(1)}, u32[]{:S(2)}, u32[]{:S(2)}) collective-permute-start(f32[2,2,512]{2,1,0:T(2,128)S(1)} %get-tuple-element.60), channel_id=1, source_target_pairs={{0,8},{8,16},{16,24},{24,0},{1,9},{9,17},{17,25},{25,1},{2,10},{10... | collective-permute-start | bytes 24584 | tf_op jit(solution)/shard_map/ppermute | solution.py:18
  89.0 3.0 %collective-permute-start.13 = (f32[2,2,512]{2,1,0:T(2,128)S(1)}, f32[2,2,512]{2,1,0:T(2,128)S(1)}, u32[]{:S(2)}, u32[]{:S(2)}) collective-permute-start(f32[2,2,512]{2,1,0:T(2,128)S(1)} %get-tuple-element.61), channel_id=1, source_target_pairs={{8,0},{16,8},{24,16},{0,24},{9,1},{17,9},{25,17},{1,25},{10,2},{18... | collective-permute-start | bytes 24584 | tf_op jit(solution)/shard_map/ppermute | solution.py:20
  92.1 9.1 %collective-permute-start.14 = (f32[2,132,2]{2,1,0:T(8,128)S(1)}, f32[2,132,2]{2,1,0:T(8,128)S(1)}, u32[]{:S(2)}, u32[]{:S(2)}) collective-permute-start(f32[2,132,2]{2,1,0:T(8,128)S(1)} %get-tuple-element.28), channel_id=1, source_target_pairs={{0,1},{1,2},{2,3},{3,4},{4,5},{5,6},{6,7},{7,0},{8,9},{9,10},{10,1... | collective-permute-start | bytes 6344 | tf_op jit(solution)/shard_map/ppermute | solution.py:18
  92.2 9.0 %collective-permute-start.15 = (f32[2,132,2]{2,1,0:T(8,128)S(1)}, f32[2,132,2]{2,1,0:T(8,128)S(1)}, u32[]{:S(2)}, u32[]{:S(2)}) collective-permute-start(f32[2,132,2]{2,1,0:T(8,128)S(1)} %get-tuple-element.29), channel_id=1, source_target_pairs={{1,0},{2,1},{3,2},{4,3},{5,4},{6,5},{7,6},{0,7},{9,8},{10,9},{11,1... | collective-permute-start | bytes 6344 | tf_op jit(solution)/shard_map/ppermute | solution.py:20
  102.5 3.1 %collective-permute-start.16 = (f32[2,2,512]{2,1,0:T(2,128)S(1)}, f32[2,2,512]{2,1,0:T(2,128)S(1)}, u32[]{:S(2)}, u32[]{:S(2)}) collective-permute-start(f32[2,2,512]{2,1,0:T(2,128)S(1)} %get-tuple-element.56), channel_id=1, source_target_pairs={{0,8},{8,16},{16,24},{24,0},{1,9},{9,17},{17,25},{25,1},{2,10},{10... | collective-permute-start | bytes 24584 | tf_op jit(solution)/shard_map/ppermute | solution.py:18
  102.9 2.7 %collective-permute-start.17 = (f32[2,2,512]{2,1,0:T(2,128)S(1)}, f32[2,2,512]{2,1,0:T(2,128)S(1)}, u32[]{:S(2)}, u32[]{:S(2)}) collective-permute-start(f32[2,2,512]{2,1,0:T(2,128)S(1)} %get-tuple-element.57), channel_id=1, source_target_pairs={{8,0},{16,8},{24,16},{0,24},{9,1},{17,9},{25,17},{1,25},{10,2},{18... | collective-permute-start | bytes 24584 | tf_op jit(solution)/shard_map/ppermute | solution.py:20
  105.8 9.0 %collective-permute-start.18 = (f32[2,132,2]{2,1,0:T(8,128)S(1)}, f32[2,132,2]{2,1,0:T(8,128)S(1)}, u32[]{:S(2)}, u32[]{:S(2)}) collective-permute-start(f32[2,132,2]{2,1,0:T(8,128)S(1)} %get-tuple-element.24), channel_id=1, source_target_pairs={{0,1},{1,2},{2,3},{3,4},{4,5},{5,6},{6,7},{7,0},{8,9},{9,10},{10,1... | collective-permute-start | bytes 6344 | tf_op jit(solution)/shard_map/ppermute | solution.py:18
  105.9 9.1 %collective-permute-start.19 = (f32[2,132,2]{2,1,0:T(8,128)S(1)}, f32[2,132,2]{2,1,0:T(8,128)S(1)}, u32[]{:S(2)}, u32[]{:S(2)}) collective-permute-start(f32[2,132,2]{2,1,0:T(8,128)S(1)} %get-tuple-element.25), channel_id=1, source_target_pairs={{1,0},{2,1},{3,2},{4,3},{5,4},{6,5},{7,6},{0,7},{9,8},{10,9},{11,1... | collective-permute-start | bytes 6344 | tf_op jit(solution)/shard_map/ppermute | solution.py:20
  116.3 3.1 %collective-permute-start.20 = (f32[2,2,512]{2,1,0:T(2,128)S(1)}, f32[2,2,512]{2,1,0:T(2,128)S(1)}, u32[]{:S(2)}, u32[]{:S(2)}) collective-permute-start(f32[2,2,512]{2,1,0:T(2,128)S(1)} %get-tuple-element.52), channel_id=1, source_target_pairs={{0,8},{8,16},{16,24},{24,0},{1,9},{9,17},{17,25},{25,1},{2,10},{10... | collective-permute-start | bytes 24584 | tf_op jit(solution)/shard_map/ppermute | solution.py:18
  116.9 2.6 %collective-permute-start.21 = (f32[2,2,512]{2,1,0:T(2,128)S(1)}, f32[2,2,512]{2,1,0:T(2,128)S(1)}, u32[]{:S(2)}, u32[]{:S(2)}) collective-permute-start(f32[2,2,512]{2,1,0:T(2,128)S(1)} %get-tuple-element.53), channel_id=1, source_target_pairs={{8,0},{16,8},{24,16},{0,24},{9,1},{17,9},{25,17},{1,25},{10,2},{18... | collective-permute-start | bytes 24584 | tf_op jit(solution)/shard_map/ppermute | solution.py:20
  119.6 9.4 %collective-permute-start.22 = (f32[2,132,2]{2,1,0:T(8,128)S(1)}, f32[2,132,2]{2,1,0:T(8,128)S(1)}, u32[]{:S(2)}, u32[]{:S(2)}) collective-permute-start(f32[2,132,2]{2,1,0:T(8,128)S(1)} %get-tuple-element.20), channel_id=1, source_target_pairs={{0,1},{1,2},{2,3},{3,4},{4,5},{5,6},{6,7},{7,0},{8,9},{9,10},{10,1... | collective-permute-start | bytes 6344 | tf_op jit(solution)/shard_map/ppermute | solution.py:18
  119.7 10.2 %collective-permute-start.23 = (f32[2,132,2]{2,1,0:T(8,128)S(1)}, f32[2,132,2]{2,1,0:T(8,128)S(1)}, u32[]{:S(2)}, u32[]{:S(2)}) collective-permute-start(f32[2,132,2]{2,1,0:T(8,128)S(1)} %get-tuple-element.21), channel_id=1, source_target_pairs={{1,0},{2,1},{3,2},{4,3},{5,4},{6,5},{7,6},{0,7},{9,8},{10,9},{11,1... | collective-permute-start | bytes 6344 | tf_op jit(solution)/shard_map/ppermute | solution.py:20
  131.2 3.1 %collective-permute-start.24 = (f32[2,2,512]{2,1,0:T(2,128)S(1)}, f32[2,2,512]{2,1,0:T(2,128)S(1)}, u32[]{:S(2)}, u32[]{:S(2)}) collective-permute-start(f32[2,2,512]{2,1,0:T(2,128)S(1)} %get-tuple-element.48), channel_id=1, source_target_pairs={{0,8},{8,16},{16,24},{24,0},{1,9},{9,17},{17,25},{25,1},{2,10},{10... | collective-permute-start | bytes 24584 | tf_op jit(solution)/shard_map/ppermute | solution.py:18
  131.4 3.0 %collective-permute-start.25 = (f32[2,2,512]{2,1,0:T(2,128)S(1)}, f32[2,2,512]{2,1,0:T(2,128)S(1)}, u32[]{:S(2)}, u32[]{:S(2)}) collective-permute-start(f32[2,2,512]{2,1,0:T(2,128)S(1)} %get-tuple-element.49), channel_id=1, source_target_pairs={{8,0},{16,8},{24,16},{0,24},{9,1},{17,9},{25,17},{1,25},{10,2},{18... | collective-permute-start | bytes 24584 | tf_op jit(solution)/shard_map/ppermute | solution.py:20
  134.5 9.0 %collective-permute-start.26 = (f32[2,132,2]{2,1,0:T(8,128)S(1)}, f32[2,132,2]{2,1,0:T(8,128)S(1)}, u32[]{:S(2)}, u32[]{:S(2)}) collective-permute-start(f32[2,132,2]{2,1,0:T(8,128)S(1)} %get-tuple-element.16), channel_id=1, source_target_pairs={{0,1},{1,2},{2,3},{3,4},{4,5},{5,6},{6,7},{7,0},{8,9},{9,10},{10,1... | collective-permute-start | bytes 6344 | tf_op jit(solution)/shard_map/ppermute | solution.py:18
  134.7 10.2 %collective-permute-start.27 = (f32[2,132,2]{2,1,0:T(8,128)S(1)}, f32[2,132,2]{2,1,0:T(8,128)S(1)}, u32[]{:S(2)}, u32[]{:S(2)}) collective-permute-start(f32[2,132,2]{2,1,0:T(8,128)S(1)} %get-tuple-element.17), channel_id=1, source_target_pairs={{1,0},{2,1},{3,2},{4,3},{5,4},{6,5},{7,6},{0,7},{9,8},{10,9},{11,1... | collective-permute-start | bytes 6344 | tf_op jit(solution)/shard_map/ppermute | solution.py:20
  146.3 3.1 %collective-permute-start.28 = (f32[2,2,512]{2,1,0:T(2,128)S(1)}, f32[2,2,512]{2,1,0:T(2,128)S(1)}, u32[]{:S(2)}, u32[]{:S(2)}) collective-permute-start(f32[2,2,512]{2,1,0:T(2,128)S(1)} %get-tuple-element.44), channel_id=1, source_target_pairs={{0,8},{8,16},{16,24},{24,0},{1,9},{9,17},{17,25},{25,1},{2,10},{10... | collective-permute-start | bytes 24584 | tf_op jit(solution)/shard_map/ppermute | solution.py:18
  146.5 3.0 %collective-permute-start.29 = (f32[2,2,512]{2,1,0:T(2,128)S(1)}, f32[2,2,512]{2,1,0:T(2,128)S(1)}, u32[]{:S(2)}, u32[]{:S(2)}) collective-permute-start(f32[2,2,512]{2,1,0:T(2,128)S(1)} %get-tuple-element.45), channel_id=1, source_target_pairs={{8,0},{16,8},{24,16},{0,24},{9,1},{17,9},{25,17},{1,25},{10,2},{18... | collective-permute-start | bytes 24584 | tf_op jit(solution)/shard_map/ppermute | solution.py:20
  149.6 9.0 %collective-permute-start.30 = (f32[2,132,2]{2,1,0:T(8,128)S(1)}, f32[2,132,2]{2,1,0:T(8,128)S(1)}, u32[]{:S(2)}, u32[]{:S(2)}) collective-permute-start(f32[2,132,2]{2,1,0:T(8,128)S(1)} %get-tuple-element.12), channel_id=1, source_target_pairs={{0,1},{1,2},{2,3},{3,4},{4,5},{5,6},{6,7},{7,0},{8,9},{9,10},{10,1... | collective-permute-start | bytes 6344 | tf_op jit(solution)/shard_map/ppermute | solution.py:18
  149.8 10.2 %collective-permute-start.31 = (f32[2,132,2]{2,1,0:T(8,128)S(1)}, f32[2,132,2]{2,1,0:T(8,128)S(1)}, u32[]{:S(2)}, u32[]{:S(2)}) collective-permute-start(f32[2,132,2]{2,1,0:T(8,128)S(1)} %get-tuple-element.13), channel_id=1, source_target_pairs={{1,0},{2,1},{3,2},{4,3},{5,4},{6,5},{7,6},{0,7},{9,8},{10,9},{11,1... | collective-permute-start | bytes 6344 | tf_op jit(solution)/shard_map/ppermute | solution.py:20
where the time goes:
time: 163 us; the launch traced here: 162 us
  starting transfers between devices  60.8 us (37%)
  waiting for transfers between devices  57.7 us (35%)
  local copies, waits for them, and re-layouts  31.8 us (20%)
  other arithmetic  11.7 us (7%)
    ppermute x16, waiting for transfers between devices, with_halo(): lax.ppermute(tail, axis, [(i, (i + 1) % count) for i in range(count)])  50.1 us
    ppermute x16, starting transfers between devices, with_halo(): lax.ppermute(head, axis, [((i + 1) % count, i) for i in range(count)])  46.3 us
    unnamed x6, local copies, waits for them, and re-layouts  24.5 us
    ppermute x16, waiting for transfers between devices, with_halo(): lax.ppermute(head, axis, [((i + 1) % count, i) for i in range(count)])  7.54 us
    ppermute x16, starting transfers between devices, with_halo(): lax.ppermute(tail, axis, [(i, (i + 1) % count) for i in range(count)])  7.29 us
    all_to_all x1, starting transfers between devices, local(): lax.all_to_all(index_panels, 'col', split_axis=2, concat_axis=1, tiled=True)  7.28 us
    all_to_all x1, local copies, waits for them, and re-layouts, local(): lax.all_to_all(index_panels, 'col', split_axis=2, concat_axis=1, tiled=True)  6.41 us
    add x8, other arithmetic, slope(): diffraction * laplace(padded)  4.96 us
  transfers between devices with their start and end apart: 33, of which 22 were waited for; matrix products, arithmetic and copies ran while one was open for 1% of the time, Pallas kernels for 0%

commit v1 on v0

--- a/solution.py
+++ b/solution.py
@@ -6,6 +6,22 @@
 STEPS = 2
 diffraction = 0.15
 phase_gain = 0.25
+
+
+def _follow_roads(here_x, row_dim, block_in):
+    arr_now = here_x.shape
+    right_arr = here_x.reshape(
+        *arr_now[:row_dim], block_in, arr_now[row_dim] // block_in, *arr_now[row_dim + 1 :]
+    )
+    front = jnp.moveaxis(right_arr, row_dim, 0)
+    return front
+
+
+def guide_squares(array_in, at_axis):
+    upper = list(array_in.shape[1:])
+    upper[at_axis] *= array_in.shape[0]
+    answer = jnp.moveaxis(array_in, 0, at_axis).reshape(upper)
+    return answer
 
 
 def with_halo(cells, sides, width):
@@ -47,7 +63,22 @@
 
 
 def local(optical_field, index_panels):
-    planes_all = lax.all_to_all(index_panels, "col", split_axis=2, concat_axis=1, tiled=True)
+
+    def play_seats_all_all(arr, mesh_dim, m, block_here):
+        part_now = lax.axis_size(mesh_dim)
+        w2, out_arr = (part_now, lax.axis_index(mesh_dim))
+        near = _follow_roads(arr, m, w2)
+        steps_seen = [near[out_arr]]
+        for d in range(1, w2):
+            x_next = near[out_arr ^ d]
+            steps_seen.append(
+                lax.ppermute(x_next, axis_name=mesh_dim, perm=[(s, s ^ d) for s in range(w2)])
+            )
+        near = jnp.stack(steps_seen)[out_arr ^ jnp.arange(w2)]
+        z2 = guide_squares(near, block_here)
+        return z2
+
+    planes_all = play_seats_all_all(index_panels, "col", 2, 1)
     field = optical_field
     planes = None
     for step_index in range(STEPS):

time: 163 us -> 145 us (0.89)
  local copies, waits for them, and re-layouts: 31.8 us -> 10.6 us
  starting transfers between devices: 60.8 us -> 65.5 us
    unnamed x6 -> x18, local copies, waits for them, and re-layouts: 24.5 us -> 5.9 us
    ppermute x0 -> x7, starting transfers between devices: none -> 12 us  [play_seats_all_all(): lax.ppermute(x_next, axis_name=mesh_dim, perm=[(s, s ^ d) for s in range(...]
    ppermute x16, waiting for transfers between devices: 50.1 us -> 41.8 us  [with_halo(): lax.ppermute(tail, axis, [(i, (i + 1) % count) for i in range(count)])]
    all_to_all x1 -> x0, starting transfers between devices: 7.28 us -> none  [local(): lax.all_to_all(index_panels, 'col', split_axis=2, concat_axis=1, tiled=True)]
    all_to_all x1 -> x0, local copies, waits for them, and re-layouts: 6.41 us -> none  [local(): lax.all_to_all(index_panels, 'col', split_axis=2, concat_axis=1, tiled=True)]
    ppermute x0 -> x7, waiting for transfers between devices: none -> 4.96 us  [play_seats_all_all(): lax.ppermute(x_next, axis_name=mesh_dim, perm=[(s, s ^ d) for s in range(...]
    another operation x0 -> x2, local copies, waits for them, and re-layouts: none -> 2.22 us
    ppermute x16, waiting for transfers between devices: 7.54 us -> 9.55 us  [with_halo(): lax.ppermute(head, axis, [((i + 1) % count, i) for i in range(count)])]
  transfers between devices with their start and end apart: 33 -> 39, of which waited for: 22 -> 23; matrix products, arithmetic and copies ran while one was open for 1% -> 5% of each run, Pallas kernels for 0% -> 0%
where the time goes in v1:
time: 145 us
  starting transfers between devices  65.5 us (45%)
  waiting for transfers between devices  56.3 us (39%)
  other arithmetic  11.7 us (8%)
  local copies, waits for them, and re-layouts  10.6 us (7%)
    ppermute x16, starting transfers between devices, with_halo(): lax.ppermute(head, axis, [((i + 1) % count, i) for i in range(count)])  47.6 us
    ppermute x16, waiting for transfers between devices, with_halo(): lax.ppermute(tail, axis, [(i, (i + 1) % count) for i in range(count)])  41.8 us
    ppermute x7, starting transfers between devices, play_seats_all_all(): lax.ppermute(x_next, axis_name=mesh_dim, perm=[(s, s ^ d) for s in range(...  12 us
    ppermute x16, waiting for transfers between devices, with_halo(): lax.ppermute(head, axis, [((i + 1) % count, i) for i in range(count)])  9.55 us
    ppermute x16, starting transfers between devices, with_halo(): lax.ppermute(tail, axis, [(i, (i + 1) % count) for i in range(count)])  5.95 us
    unnamed x18, local copies, waits for them, and re-layouts  5.9 us
    add x8, other arithmetic, slope(): diffraction * laplace(padded)  4.96 us
    ppermute x7, waiting for transfers between devices, play_seats_all_all(): lax.ppermute(x_next, axis_name=mesh_dim, perm=[(s, s ^ d) for s in range(...  4.96 us
  transfers between devices with their start and end apart: 39, of which 23 were waited for; matrix products, arithmetic and copies ran while one was open for 5% of the time, Pallas kernels for 0%

profile of v1, /device:TPU:0, one launch (start us, length us, event | category | flops | bytes accessed | tf_op | source)
XLA Modules:
  0.0 144.7 jit_solution(11211464724781880597)
XLA Ops:
  0.8 2.4 %collective-permute-start.1 = (f32[2,2,512]{2,1,0:T(2,128)S(1)}, f32[2,2,512]{2,1,0:T(2,128)S(1)}, u32[]{:S(2)}, u32[]{:S(2)}) collective-permute-start(f32[2,2,512]{2,1,0:T(2,128)S(1)} %get-tuple-element.80), channel_id=1, source_target_pairs={{8,0},{16,8},{24,16},{0,24},{9,1},{17,9},{25,17},{1,25},{10,2},{18... | collective-permute-start | bytes 24584 | tf_op jit(solution)/shard_map/ppermute | solution.py:36
  3.2 1.3 copy.11
  4.5 1.6 %constant_dynamic-slice_fusion = (bf16[5,16,1,512]{3,2,1,0:T(2,128)(2,1)S(1)}, bf16[5,16,1,512]{3,2,1,0:T(2,128)(2,1)S(1)}, bf16[5,16,1,512]{3,2,1,0:T(2,128)(2,...) fusion(bf16[5,16,8,512]{3,2,1,0:T(8,128)(2,1)S(1)} %bitcast.49,, ...), kind=kLoop, calls=%fused_computation.247 | loop fusion | bytes 1310752 | tf_op jit(solution)/shard_map/dynamic-slice.7
  6.2 1.6 %collective-permute-start.4 = (bf16[5,16,512]{2,1,0:T(8,128)(2,1)S(1)}, bf16[5,16,512]{2,1,0:T(8,128)(2,1)S(1)}, u32[]{:S(2)}, u32[]{:S(2)}) collective-permute-start(bf16[5,16,512]{2,1,0:T(8,128)(2,1)S(1)} %bitcast.65), channel_id=1, source_target_pairs={{0,1},{1,0},{2,3},{3,2},{4,5},{5,4},{6,7},{7,6},{8,9},{9,8},{10,11... | collective-permute-start | bytes 245768 | tf_op jit(solution)/shard_map/ppermute | solution.py:75
  7.8 1.6 %collective-permute-start.5 = (bf16[5,16,512]{2,1,0:T(8,128)(2,1)S(1)}, bf16[5,16,512]{2,1,0:T(8,128)(2,1)S(1)}, u32[]{:S(2)}, u32[]{:S(2)}) collective-permute-start(bf16[5,16,512]{2,1,0:T(8,128)(2,1)S(1)} %bitcast.64), channel_id=1, source_target_pairs={{0,2},{1,3},{2,0},{3,1},{4,6},{5,7},{6,4},{7,5},{8,10},{9,11},{10,... | collective-permute-start | bytes 245768 | tf_op jit(solution)/shard_map/ppermute | solution.py:75
  10.8 1.6 %collective-permute-start.2 = (f32[2,132,2]{2,1,0:T(8,128)S(1)}, f32[2,132,2]{2,1,0:T(8,128)S(1)}, u32[]{:S(2)}, u32[]{:S(2)}) collective-permute-start(f32[2,132,2]{2,1,0:T(8,128)S(1)} %get-tuple-element.48), channel_id=1, source_target_pairs={{0,1},{1,2},{2,3},{3,4},{4,5},{5,6},{6,7},{7,0},{8,9},{9,10},{10,1... | collective-permute-start | bytes 6344 | tf_op jit(solution)/shard_map/ppermute | solution.py:34
  12.4 3.2 %collective-permute-start.3 = (f32[2,132,2]{2,1,0:T(8,128)S(1)}, f32[2,132,2]{2,1,0:T(8,128)S(1)}, u32[]{:S(2)}, u32[]{:S(2)}) collective-permute-start(f32[2,132,2]{2,1,0:T(8,128)S(1)} %get-tuple-element.49), channel_id=1, source_target_pairs={{1,0},{2,1},{3,2},{4,3},{5,4},{6,5},{7,6},{0,7},{9,8},{10,9},{11,1... | collective-permute-start | bytes 6344 | tf_op jit(solution)/shard_map/ppermute | solution.py:36
  15.6 4.4 %collective-permute-done.2 = f32[2,132,2]{2,1,0:T(8,128)S(1)} collective-permute-done((f32[2,132,2]{2,1,0:T(8,128)S(1)}, f32[2,132,2]{2,1,0:T(8,128)S(1)}, u32[]{:S(2)}, u32[]{:S(2)}) %collective-permute-start.2) | collective-permute-done | bytes 2144 | tf_op jit(solution)/shard_map/ppermute | solution.py:34
  20.1 1.9 %collective-permute-start.7 = (bf16[5,16,512]{2,1,0:T(8,128)(2,1)S(1)}, bf16[5,16,512]{2,1,0:T(8,128)(2,1)S(1)}, u32[]{:S(2)}, u32[]{:S(2)}) collective-permute-start(bf16[5,16,512]{2,1,0:T(8,128)(2,1)S(1)} %bitcast.66), channel_id=1, source_target_pairs={{0,4},{1,5},{2,6},{3,7},{4,0},{5,1},{6,2},{7,3},{8,12},{9,13},{10,... | collective-permute-start | bytes 245768 | tf_op jit(solution)/shard_map/ppermute | solution.py:75
  22.0 2.3 %collective-permute-start.8 = (bf16[5,16,512]{2,1,0:T(8,128)(2,1)S(1)}, bf16[5,16,512]{2,1,0:T(8,128)(2,1)S(1)}, u32[]{:S(2)}, u32[]{:S(2)}) collective-permute-start(bf16[5,16,512]{2,1,0:T(8,128)(2,1)S(1)} %bitcast.63), channel_id=1, source_target_pairs={{0,5},{1,4},{2,7},{3,6},{4,1},{5,0},{6,3},{7,2},{8,13},{9,12},{10,... | collective-permute-start | bytes 245768 | tf_op jit(solution)/shard_map/ppermute | solution.py:75
  24.5 3.7 %collective-permute-start.9 = (bf16[5,16,512]{2,1,0:T(8,128)(2,1)S(1)}, bf16[5,16,512]{2,1,0:T(8,128)(2,1)S(1)}, u32[]{:S(2)}, u32[]{:S(2)}) collective-permute-start(bf16[5,16,512]{2,1,0:T(8,128)(2,1)S(1)} %bitcast.61), channel_id=1, source_target_pairs={{0,6},{1,7},{2,4},{3,5},{4,2},{5,3},{6,0},{7,1},{8,14},{9,15},{10,... | collective-permute-start | bytes 245768 | tf_op jit(solution)/shard_map/ppermute | solution.py:75
  31.2 4.9 %collective-permute-done.8 = bf16[5,16,512]{2,1,0:T(8,128)(2,1)S(1)} collective-permute-done((bf16[5,16,512]{2,1,0:T(8,128)(2,1)S(1)}, bf16[5,16,512]{2,1,0:T(8,128)(2,1)S(1)}, u32[]{:S(2)}, u32[]{:S(2)}) %collective-permute-start.8) | collective-permute-done | bytes 81952 | tf_op jit(solution)/shard_map/ppermute | solution.py:75
  38.0 1.7 %gather_fusion = bf16[8,5,16,512]{3,2,1,0:T(8,128)(2,1)S(1)} fusion(bf16[8,5,16,512]{3,2,1,0:T(8,128)(2,1)} %bitcast_dynamic-update-slice_fusion.1, s32[1024]{0:T(1024)S(1)} %pad_clamp_fusion), kind=kCustom, calls=%fused_computation | custom fusion | bytes 1310752 | tf_op jit(solution)/shard_map/gather | solution.py:77
  40.7 1.7 %collective-permute-start.12 = (f32[2,2,512]{2,1,0:T(2,128)S(1)}, f32[2,2,512]{2,1,0:T(2,128)S(1)}, u32[]{:S(2)}, u32[]{:S(2)}) collective-permute-start(f32[2,2,512]{2,1,0:T(2,128)S(1)} %get-tuple-element.77), channel_id=1, source_target_pairs={{8,0},{16,8},{24,16},{0,24},{9,1},{17,9},{25,17},{1,25},{10,2},{18... | collective-permute-start | bytes 24584 | tf_op jit(solution)/shard_map/ppermute | solution.py:36
  42.5 1.3 collective-permute-done.11
  44.6 4.1 %collective-permute-start.14 = (f32[2,132,2]{2,1,0:T(8,128)S(1)}, f32[2,132,2]{2,1,0:T(8,128)S(1)}, u32[]{:S(2)}, u32[]{:S(2)}) collective-permute-start(f32[2,132,2]{2,1,0:T(8,128)S(1)} %get-tuple-element.45), channel_id=1, source_target_pairs={{1,0},{2,1},{3,2},{4,3},{5,4},{6,5},{7,6},{0,7},{9,8},{10,9},{11,1... | collective-permute-start | bytes 6344 | tf_op jit(solution)/shard_map/ppermute | solution.py:36
  48.7 4.2 %collective-permute-done.13 = f32[2,132,2]{2,1,0:T(8,128)S(1)} collective-permute-done((f32[2,132,2]{2,1,0:T(8,128)S(1)}, f32[2,132,2]{2,1,0:T(8,128)S(1)}, u32[]{:S(2)}, u32[]{:S(2)}) %collective-permute-start.13) | collective-permute-done | bytes 2144 | tf_op jit(solution)/shard_map/ppermute | solution.py:34
  53.0 1.7 %collective-permute-done.14 = f32[2,132,2]{2,1,0:T(8,128)S(1)} collective-permute-done((f32[2,132,2]{2,1,0:T(8,128)S(1)}, f32[2,132,2]{2,1,0:T(8,128)S(1)}, u32[]{:S(2)}, u32[]{:S(2)}) %collective-permute-start.14) | collective-permute-done | bytes 2144 | tf_op jit(solution)/shard_map/ppermute | solution.py:36
  56.0 1.5 %collective-permute-start.16 = (f32[2,2,512]{2,1,0:T(2,128)S(1)}, f32[2,2,512]{2,1,0:T(2,128)S(1)}, u32[]{:S(2)}, u32[]{:S(2)}) collective-permute-start(f32[2,2,512]{2,1,0:T(2,128)S(1)} %get-tuple-element.73), channel_id=1, source_target_pairs={{8,0},{16,8},{24,16},{0,24},{9,1},{17,9},{25,17},{1,25},{10,2},{18... | collective-permute-start | bytes 24584 | tf_op jit(solution)/shard_map/ppermute | solution.py:36
  57.5 1.3 collective-permute-done.15
  59.2 4.6 %collective-permute-start.18 = (f32[2,132,2]{2,1,0:T(8,128)S(1)}, f32[2,132,2]{2,1,0:T(8,128)S(1)}, u32[]{:S(2)}, u32[]{:S(2)}) collective-permute-start(f32[2,132,2]{2,1,0:T(8,128)S(1)} %get-tuple-element.41), channel_id=1, source_target_pairs={{1,0},{2,1},{3,2},{4,3},{5,4},{6,5},{7,6},{0,7},{9,8},{10,9},{11,1... | collective-permute-start | bytes 6344 | tf_op jit(solution)/shard_map/ppermute | solution.py:36
  63.8 4.0 %collective-permute-done.17 = f32[2,132,2]{2,1,0:T(8,128)S(1)} collective-permute-done((f32[2,132,2]{2,1,0:T(8,128)S(1)}, f32[2,132,2]{2,1,0:T(8,128)S(1)}, u32[]{:S(2)}, u32[]{:S(2)}) %collective-permute-start.17) | collective-permute-done | bytes 2144 | tf_op jit(solution)/shard_map/ppermute | solution.py:34
  67.8 1.8 %collective-permute-done.18 = f32[2,132,2]{2,1,0:T(8,128)S(1)} collective-permute-done((f32[2,132,2]{2,1,0:T(8,128)S(1)}, f32[2,132,2]{2,1,0:T(8,128)S(1)}, u32[]{:S(2)}, u32[]{:S(2)}) %collective-permute-start.18) | collective-permute-done | bytes 2144 | tf_op jit(solution)/shard_map/ppermute | solution.py:36
  70.8 1.6 %collective-permute-start.20 = (f32[2,2,512]{2,1,0:T(2,128)S(1)}, f32[2,2,512]{2,1,0:T(2,128)S(1)}, u32[]{:S(2)}, u32[]{:S(2)}) collective-permute-start(f32[2,2,512]{2,1,0:T(2,128)S(1)} %get-tuple-element.69), channel_id=1, source_target_pairs={{8,0},{16,8},{24,16},{0,24},{9,1},{17,9},{25,17},{1,25},{10,2},{18... | collective-permute-start | bytes 24584 | tf_op jit(solution)/shard_map/ppermute | solution.py:36
  72.4 1.3 collective-permute-done.19
  74.2 4.5 %collective-permute-start.22 = (f32[2,132,2]{2,1,0:T(8,128)S(1)}, f32[2,132,2]{2,1,0:T(8,128)S(1)}, u32[]{:S(2)}, u32[]{:S(2)}) collective-permute-start(f32[2,132,2]{2,1,0:T(8,128)S(1)} %get-tuple-element.37), channel_id=1, source_target_pairs={{1,0},{2,1},{3,2},{4,3},{5,4},{6,5},{7,6},{0,7},{9,8},{10,9},{11,1... | collective-permute-start | bytes 6344 | tf_op jit(solution)/shard_map/ppermute | solution.py:36
  78.7 4.1 %collective-permute-done.21 = f32[2,132,2]{2,1,0:T(8,128)S(1)} collective-permute-done((f32[2,132,2]{2,1,0:T(8,128)S(1)}, f32[2,132,2]{2,1,0:T(8,128)S(1)}, u32[]{:S(2)}, u32[]{:S(2)}) %collective-permute-start.21) | collective-permute-done | bytes 2144 | tf_op jit(solution)/shard_map/ppermute | solution.py:34
  82.8 1.2 collective-permute-done.22
  85.5 1.6 %collective-permute-start.24 = (f32[2,2,512]{2,1,0:T(2,128)S(1)}, f32[2,2,512]{2,1,0:T(2,128)S(1)}, u32[]{:S(2)}, u32[]{:S(2)}) collective-permute-start(f32[2,2,512]{2,1,0:T(2,128)S(1)} %get-tuple-element.65), channel_id=1, source_target_pairs={{8,0},{16,8},{24,16},{0,24},{9,1},{17,9},{25,17},{1,25},{10,2},{18... | collective-permute-start | bytes 24584 | tf_op jit(solution)/shard_map/ppermute | solution.py:36
  87.2 1.3 collective-permute-done.23
  88.8 4.6 %collective-permute-start.26 = (f32[2,132,2]{2,1,0:T(8,128)S(1)}, f32[2,132,2]{2,1,0:T(8,128)S(1)}, u32[]{:S(2)}, u32[]{:S(2)}) collective-permute-start(f32[2,132,2]{2,1,0:T(8,128)S(1)} %get-tuple-element.33), channel_id=1, source_target_pairs={{1,0},{2,1},{3,2},{4,3},{5,4},{6,5},{7,6},{0,7},{9,8},{10,9},{11,1... | collective-permute-start | bytes 6344 | tf_op jit(solution)/shard_map/ppermute | solution.py:36
  93.4 4.1 %collective-permute-done.25 = f32[2,132,2]{2,1,0:T(8,128)S(1)} collective-permute-done((f32[2,132,2]{2,1,0:T(8,128)S(1)}, f32[2,132,2]{2,1,0:T(8,128)S(1)}, u32[]{:S(2)}, u32[]{:S(2)}) %collective-permute-start.25) | collective-permute-done | bytes 2144 | tf_op jit(solution)/shard_map/ppermute | solution.py:34
  99.6 1.1 collective-permute-start.28
  100.7 1.3 collective-permute-done.27
  102.8 4.6 %collective-permute-start.30 = (f32[2,132,2]{2,1,0:T(8,128)S(1)}, f32[2,132,2]{2,1,0:T(8,128)S(1)}, u32[]{:S(2)}, u32[]{:S(2)}) collective-permute-start(f32[2,132,2]{2,1,0:T(8,128)S(1)} %get-tuple-element.29), channel_id=1, source_target_pairs={{1,0},{2,1},{3,2},{4,3},{5,4},{6,5},{7,6},{0,7},{9,8},{10,9},{11,1... | collective-permute-start | bytes 6344 | tf_op jit(solution)/shard_map/ppermute | solution.py:36
  107.3 3.5 %collective-permute-done.29 = f32[2,132,2]{2,1,0:T(8,128)S(1)} collective-permute-done((f32[2,132,2]{2,1,0:T(8,128)S(1)}, f32[2,132,2]{2,1,0:T(8,128)S(1)}, u32[]{:S(2)}, u32[]{:S(2)}) %collective-permute-start.29) | collective-permute-done | bytes 2144 | tf_op jit(solution)/shard_map/ppermute | solution.py:34
  110.9 0.9 collective-permute-done.30
  113.6 1.3 collective-permute-start.32
  115.0 1.3 collective-permute-done.31
  116.7 4.5 %collective-permute-start.34 = (f32[2,132,2]{2,1,0:T(8,128)S(1)}, f32[2,132,2]{2,1,0:T(8,128)S(1)}, u32[]{:S(2)}, u32[]{:S(2)}) collective-permute-start(f32[2,132,2]{2,1,0:T(8,128)S(1)} %get-tuple-element.25), channel_id=1, source_target_pairs={{1,0},{2,1},{3,2},{4,3},{5,4},{6,5},{7,6},{0,7},{9,8},{10,9},{11,1... | collective-permute-start | bytes 6344 | tf_op jit(solution)/shard_map/ppermute | solution.py:36
  121.2 3.8 %collective-permute-done.33 = f32[2,132,2]{2,1,0:T(8,128)S(1)} collective-permute-done((f32[2,132,2]{2,1,0:T(8,128)S(1)}, f32[2,132,2]{2,1,0:T(8,128)S(1)}, u32[]{:S(2)}, u32[]{:S(2)}) %collective-permute-start.33) | collective-permute-done | bytes 2144 | tf_op jit(solution)/shard_map/ppermute | solution.py:34
  125.1 2.2 %collective-permute-done.34 = f32[2,132,2]{2,1,0:T(8,128)S(1)} collective-permute-done((f32[2,132,2]{2,1,0:T(8,128)S(1)}, f32[2,132,2]{2,1,0:T(8,128)S(1)}, u32[]{:S(2)}, u32[]{:S(2)}) %collective-permute-start.34) | collective-permute-done | bytes 2144 | tf_op jit(solution)/shard_map/ppermute | solution.py:36
  128.8 1.6 %collective-permute-start.36 = (f32[2,2,512]{2,1,0:T(2,128)S(1)}, f32[2,2,512]{2,1,0:T(2,128)S(1)}, u32[]{:S(2)}, u32[]{:S(2)}) collective-permute-start(f32[2,2,512]{2,1,0:T(2,128)S(1)} %get-tuple-element.53), channel_id=1, source_target_pairs={{8,0},{16,8},{24,16},{0,24},{9,1},{17,9},{25,17},{1,25},{10,2},{18... | collective-permute-start | bytes 24584 | tf_op jit(solution)/shard_map/ppermute | solution.py:36
  130.4 1.3 collective-permute-done.35
  132.1 4.5 %collective-permute-start.38 = (f32[2,132,2]{2,1,0:T(8,128)S(1)}, f32[2,132,2]{2,1,0:T(8,128)S(1)}, u32[]{:S(2)}, u32[]{:S(2)}) collective-permute-start(f32[2,132,2]{2,1,0:T(8,128)S(1)} %get-tuple-element.21), channel_id=1, source_target_pairs={{1,0},{2,1},{3,2},{4,3},{5,4},{6,5},{7,6},{0,7},{9,8},{10,9},{11,1... | collective-permute-start | bytes 6344 | tf_op jit(solution)/shard_map/ppermute | solution.py:36
  136.7 4.2 %collective-permute-done.37 = f32[2,132,2]{2,1,0:T(8,128)S(1)} collective-permute-done((f32[2,132,2]{2,1,0:T(8,128)S(1)}, f32[2,132,2]{2,1,0:T(8,128)S(1)}, u32[]{:S(2)}, u32[]{:S(2)}) %collective-permute-start.37) | collective-permute-done | bytes 2144 | tf_op jit(solution)/shard_map/ppermute | solution.py:34
  140.8 1.5 %collective-permute-done.38 = f32[2,132,2]{2,1,0:T(8,128)S(1)} collective-permute-done((f32[2,132,2]{2,1,0:T(8,128)S(1)}, f32[2,132,2]{2,1,0:T(8,128)S(1)}, u32[]{:S(2)}, u32[]{:S(2)}) %collective-permute-start.38) | collective-permute-done | bytes 2144 | tf_op jit(solution)/shard_map/ppermute | solution.py:36
  143.3 1.4 fusion.97
  (103 shorter events, 22.1 us)
Async XLA Ops:
  0.8 9.9 %collective-permute-start.1 = (f32[2,2,512]{2,1,0:T(2,128)S(1)}, f32[2,2,512]{2,1,0:T(2,128)S(1)}, u32[]{:S(2)}, u32[]{:S(2)}) collective-permute-start(f32[2,2,512]{2,1,0:T(2,128)S(1)} %get-tuple-element.80), channel_id=1, source_target_pairs={{8,0},{16,8},{24,16},{0,24},{9,1},{17,9},{25,17},{1,25},{10,2},{18... | collective-permute-start | bytes 24584 | tf_op jit(solution)/shard_map/ppermute | solution.py:36
  3.2 7.5 %collective-permute-start = (f32[2,2,512]{2,1,0:T(2,128)S(1)}, f32[2,2,512]{2,1,0:T(2,128)S(1)}, u32[]{:S(2)}, u32[]{:S(2)}) collective-permute-start(f32[2,2,512]{2,1,0:T(2,128)S(1)} %get-tuple-element.81), channel_id=1, source_target_pairs={{0,8},{8,16},{16,24},{24,0},{1,9},{9,17},{17,25},{25,1},{2,10},{10... | collective-permute-start | bytes 24584 | tf_op jit(solution)/shard_map/ppermute | solution.py:34
  6.1 3.8 %copy-start = (f32[2,128,512]{2,1,0:T(8,128)S(1)}, f32[2,128,512]{2,1,0:T(8,128)}, u32[]{:S(2)}) copy-start(f32[2,128,512]{2,1,0:T(8,128)} %param.2) | copy-start | bytes 1572868
  6.2 18.3 %collective-permute-start.4 = (bf16[5,16,512]{2,1,0:T(8,128)(2,1)S(1)}, bf16[5,16,512]{2,1,0:T(8,128)(2,1)S(1)}, u32[]{:S(2)}, u32[]{:S(2)}) collective-permute-start(bf16[5,16,512]{2,1,0:T(8,128)(2,1)S(1)} %bitcast.65), channel_id=1, source_target_pairs={{0,1},{1,0},{2,3},{3,2},{4,5},{5,4},{6,7},{7,6},{8,9},{9,8},{10,11... | collective-permute-start | bytes 245768 | tf_op jit(solution)/shard_map/ppermute | solution.py:75
  7.8 21.0 %collective-permute-start.5 = (bf16[5,16,512]{2,1,0:T(8,128)(2,1)S(1)}, bf16[5,16,512]{2,1,0:T(8,128)(2,1)S(1)}, u32[]{:S(2)}, u32[]{:S(2)}) collective-permute-start(bf16[5,16,512]{2,1,0:T(8,128)(2,1)S(1)} %bitcast.64), channel_id=1, source_target_pairs={{0,2},{1,3},{2,0},{3,1},{4,6},{5,7},{6,4},{7,5},{8,10},{9,11},{10,... | collective-permute-start | bytes 245768 | tf_op jit(solution)/shard_map/ppermute | solution.py:75
  9.4 20.5 %collective-permute-start.6 = (bf16[5,16,512]{2,1,0:T(8,128)(2,1)S(1)}, bf16[5,16,512]{2,1,0:T(8,128)(2,1)S(1)}, u32[]{:S(2)}, u32[]{:S(2)}) collective-permute-start(bf16[5,16,512]{2,1,0:T(8,128)(2,1)S(1)} %bitcast.62), channel_id=1, source_target_pairs={{0,3},{1,2},{2,1},{3,0},{4,7},{5,6},{6,5},{7,4},{8,11},{9,10},{10,... | collective-permute-start | bytes 245768 | tf_op jit(solution)/shard_map/ppermute | solution.py:75
  10.8 9.2 %collective-permute-start.2 = (f32[2,132,2]{2,1,0:T(8,128)S(1)}, f32[2,132,2]{2,1,0:T(8,128)S(1)}, u32[]{:S(2)}, u32[]{:S(2)}) collective-permute-start(f32[2,132,2]{2,1,0:T(8,128)S(1)} %get-tuple-element.48), channel_id=1, source_target_pairs={{0,1},{1,2},{2,3},{3,4},{4,5},{5,6},{6,7},{7,0},{8,9},{9,10},{10,1... | collective-permute-start | bytes 6344 | tf_op jit(solution)/shard_map/ppermute | solution.py:34
  12.4 9.5 %collective-permute-start.3 = (f32[2,132,2]{2,1,0:T(8,128)S(1)}, f32[2,132,2]{2,1,0:T(8,128)S(1)}, u32[]{:S(2)}, u32[]{:S(2)}) collective-permute-start(f32[2,132,2]{2,1,0:T(8,128)S(1)} %get-tuple-element.49), channel_id=1, source_target_pairs={{1,0},{2,1},{3,2},{4,3},{5,4},{6,5},{7,6},{0,7},{9,8},{10,9},{11,1... | collective-permute-start | bytes 6344 | tf_op jit(solution)/shard_map/ppermute | solution.py:36
  20.1 10.5 %collective-permute-start.7 = (bf16[5,16,512]{2,1,0:T(8,128)(2,1)S(1)}, bf16[5,16,512]{2,1,0:T(8,128)(2,1)S(1)}, u32[]{:S(2)}, u32[]{:S(2)}) collective-permute-start(bf16[5,16,512]{2,1,0:T(8,128)(2,1)S(1)} %bitcast.66), channel_id=1, source_target_pairs={{0,4},{1,5},{2,6},{3,7},{4,0},{5,1},{6,2},{7,3},{8,12},{9,13},{10,... | collective-permute-start | bytes 245768 | tf_op jit(solution)/shard_map/ppermute | solution.py:75
  22.0 14.2 %collective-permute-start.8 = (bf16[5,16,512]{2,1,0:T(8,128)(2,1)S(1)}, bf16[5,16,512]{2,1,0:T(8,128)(2,1)S(1)}, u32[]{:S(2)}, u32[]{:S(2)}) collective-permute-start(bf16[5,16,512]{2,1,0:T(8,128)(2,1)S(1)} %bitcast.63), channel_id=1, source_target_pairs={{0,5},{1,4},{2,7},{3,6},{4,1},{5,0},{6,3},{7,2},{8,13},{9,12},{10,... | collective-permute-start | bytes 245768 | tf_op jit(solution)/shard_map/ppermute | solution.py:75
  24.5 12.2 %collective-permute-start.9 = (bf16[5,16,512]{2,1,0:T(8,128)(2,1)S(1)}, bf16[5,16,512]{2,1,0:T(8,128)(2,1)S(1)}, u32[]{:S(2)}, u32[]{:S(2)}) collective-permute-start(bf16[5,16,512]{2,1,0:T(8,128)(2,1)S(1)} %bitcast.61), channel_id=1, source_target_pairs={{0,6},{1,7},{2,4},{3,5},{4,2},{5,3},{6,0},{7,1},{8,14},{9,15},{10,... | collective-permute-start | bytes 245768 | tf_op jit(solution)/shard_map/ppermute | solution.py:75
  28.8 8.6 %collective-permute-start.10 = (bf16[5,16,512]{2,1,0:T(8,128)(2,1)S(1)}, bf16[5,16,512]{2,1,0:T(8,128)(2,1)S(1)}, u32[]{:S(2)}, u32[]{:S(2)}) collective-permute-start(bf16[5,16,512]{2,1,0:T(8,128)(2,1)S(1)} %bitcast.60), channel_id=1, source_target_pairs={{0,7},{1,6},{2,5},{3,4},{4,3},{5,2},{6,1},{7,0},{8,15},{9,14},{10,... | collective-permute-start | bytes 245768 | tf_op jit(solution)/shard_map/ppermute | solution.py:75
  40.7 3.1 %collective-permute-start.11 = (f32[2,2,512]{2,1,0:T(2,128)S(1)}, f32[2,2,512]{2,1,0:T(2,128)S(1)}, u32[]{:S(2)}, u32[]{:S(2)}) collective-permute-start(f32[2,2,512]{2,1,0:T(2,128)S(1)} %get-tuple-element.76), channel_id=1, source_target_pairs={{0,8},{8,16},{16,24},{24,0},{1,9},{9,17},{17,25},{25,1},{2,10},{10... | collective-permute-start | bytes 24584 | tf_op jit(solution)/shard_map/ppermute | solution.py:34
  40.7 3.1 %collective-permute-start.12 = (f32[2,2,512]{2,1,0:T(2,128)S(1)}, f32[2,2,512]{2,1,0:T(2,128)S(1)}, u32[]{:S(2)}, u32[]{:S(2)}) collective-permute-start(f32[2,2,512]{2,1,0:T(2,128)S(1)} %get-tuple-element.77), channel_id=1, source_target_pairs={{8,0},{16,8},{24,16},{0,24},{9,1},{17,9},{25,17},{1,25},{10,2},{18... | collective-permute-start | bytes 24584 | tf_op jit(solution)/shard_map/ppermute | solution.py:36
  44.0 9.0 %collective-permute-start.13 = (f32[2,132,2]{2,1,0:T(8,128)S(1)}, f32[2,132,2]{2,1,0:T(8,128)S(1)}, u32[]{:S(2)}, u32[]{:S(2)}) collective-permute-start(f32[2,132,2]{2,1,0:T(8,128)S(1)} %get-tuple-element.44), channel_id=1, source_target_pairs={{0,1},{1,2},{2,3},{3,4},{4,5},{5,6},{6,7},{7,0},{8,9},{9,10},{10,1... | collective-permute-start | bytes 6344 | tf_op jit(solution)/shard_map/ppermute | solution.py:34
  44.6 10.0 %collective-permute-start.14 = (f32[2,132,2]{2,1,0:T(8,128)S(1)}, f32[2,132,2]{2,1,0:T(8,128)S(1)}, u32[]{:S(2)}, u32[]{:S(2)}) collective-permute-start(f32[2,132,2]{2,1,0:T(8,128)S(1)} %get-tuple-element.45), channel_id=1, source_target_pairs={{1,0},{2,1},{3,2},{4,3},{5,4},{6,5},{7,6},{0,7},{9,8},{10,9},{11,1... | collective-permute-start | bytes 6344 | tf_op jit(solution)/shard_map/ppermute | solution.py:36
  55.7 3.1 %collective-permute-start.15 = (f32[2,2,512]{2,1,0:T(2,128)S(1)}, f32[2,2,512]{2,1,0:T(2,128)S(1)}, u32[]{:S(2)}, u32[]{:S(2)}) collective-permute-start(f32[2,2,512]{2,1,0:T(2,128)S(1)} %get-tuple-element.72), channel_id=1, source_target_pairs={{0,8},{8,16},{16,24},{24,0},{1,9},{9,17},{17,25},{25,1},{2,10},{10... | collective-permute-start | bytes 24584 | tf_op jit(solution)/shard_map/ppermute | solution.py:34
  56.0 2.9 %collective-permute-start.16 = (f32[2,2,512]{2,1,0:T(2,128)S(1)}, f32[2,2,512]{2,1,0:T(2,128)S(1)}, u32[]{:S(2)}, u32[]{:S(2)}) collective-permute-start(f32[2,2,512]{2,1,0:T(2,128)S(1)} %get-tuple-element.73), channel_id=1, source_target_pairs={{8,0},{16,8},{24,16},{0,24},{9,1},{17,9},{25,17},{1,25},{10,2},{18... | collective-permute-start | bytes 24584 | tf_op jit(solution)/shard_map/ppermute | solution.py:36
  59.0 8.8 %collective-permute-start.17 = (f32[2,132,2]{2,1,0:T(8,128)S(1)}, f32[2,132,2]{2,1,0:T(8,128)S(1)}, u32[]{:S(2)}, u32[]{:S(2)}) collective-permute-start(f32[2,132,2]{2,1,0:T(8,128)S(1)} %get-tuple-element.40), channel_id=1, source_target_pairs={{0,1},{1,2},{2,3},{3,4},{4,5},{5,6},{6,7},{7,0},{8,9},{9,10},{10,1... | collective-permute-start | bytes 6344 | tf_op jit(solution)/shard_map/ppermute | solution.py:34
  59.2 10.4 %collective-permute-start.18 = (f32[2,132,2]{2,1,0:T(8,128)S(1)}, f32[2,132,2]{2,1,0:T(8,128)S(1)}, u32[]{:S(2)}, u32[]{:S(2)}) collective-permute-start(f32[2,132,2]{2,1,0:T(8,128)S(1)} %get-tuple-element.41), channel_id=1, source_target_pairs={{1,0},{2,1},{3,2},{4,3},{5,4},{6,5},{7,6},{0,7},{9,8},{10,9},{11,1... | collective-permute-start | bytes 6344 | tf_op jit(solution)/shard_map/ppermute | solution.py:36
  70.6 3.1 %collective-permute-start.19 = (f32[2,2,512]{2,1,0:T(2,128)S(1)}, f32[2,2,512]{2,1,0:T(2,128)S(1)}, u32[]{:S(2)}, u32[]{:S(2)}) collective-permute-start(f32[2,2,512]{2,1,0:T(2,128)S(1)} %get-tuple-element.68), channel_id=1, source_target_pairs={{0,8},{8,16},{16,24},{24,0},{1,9},{9,17},{17,25},{25,1},{2,10},{10... | collective-permute-start | bytes 24584 | tf_op jit(solution)/shard_map/ppermute | solution.py:34
  70.8 3.0 %collective-permute-start.20 = (f32[2,2,512]{2,1,0:T(2,128)S(1)}, f32[2,2,512]{2,1,0:T(2,128)S(1)}, u32[]{:S(2)}, u32[]{:S(2)}) collective-permute-start(f32[2,2,512]{2,1,0:T(2,128)S(1)} %get-tuple-element.69), channel_id=1, source_target_pairs={{8,0},{16,8},{24,16},{0,24},{9,1},{17,9},{25,17},{1,25},{10,2},{18... | collective-permute-start | bytes 24584 | tf_op jit(solution)/shard_map/ppermute | solution.py:36
  73.9 8.9 %collective-permute-start.21 = (f32[2,132,2]{2,1,0:T(8,128)S(1)}, f32[2,132,2]{2,1,0:T(8,128)S(1)}, u32[]{:S(2)}, u32[]{:S(2)}) collective-permute-start(f32[2,132,2]{2,1,0:T(8,128)S(1)} %get-tuple-element.36), channel_id=1, source_target_pairs={{0,1},{1,2},{2,3},{3,4},{4,5},{5,6},{6,7},{7,0},{8,9},{9,10},{10,1... | collective-permute-start | bytes 6344 | tf_op jit(solution)/shard_map/ppermute | solution.py:34
  74.2 9.9 %collective-permute-start.22 = (f32[2,132,2]{2,1,0:T(8,128)S(1)}, f32[2,132,2]{2,1,0:T(8,128)S(1)}, u32[]{:S(2)}, u32[]{:S(2)}) collective-permute-start(f32[2,132,2]{2,1,0:T(8,128)S(1)} %get-tuple-element.37), channel_id=1, source_target_pairs={{1,0},{2,1},{3,2},{4,3},{5,4},{6,5},{7,6},{0,7},{9,8},{10,9},{11,1... | collective-permute-start | bytes 6344 | tf_op jit(solution)/shard_map/ppermute | solution.py:36
  85.4 3.1 %collective-permute-start.23 = (f32[2,2,512]{2,1,0:T(2,128)S(1)}, f32[2,2,512]{2,1,0:T(2,128)S(1)}, u32[]{:S(2)}, u32[]{:S(2)}) collective-permute-start(f32[2,2,512]{2,1,0:T(2,128)S(1)} %get-tuple-element.64), channel_id=1, source_target_pairs={{0,8},{8,16},{16,24},{24,0},{1,9},{9,17},{17,25},{25,1},{2,10},{10... | collective-permute-start | bytes 24584 | tf_op jit(solution)/shard_map/ppermute | solution.py:34
  85.5 3.0 %collective-permute-start.24 = (f32[2,2,512]{2,1,0:T(2,128)S(1)}, f32[2,2,512]{2,1,0:T(2,128)S(1)}, u32[]{:S(2)}, u32[]{:S(2)}) collective-permute-start(f32[2,2,512]{2,1,0:T(2,128)S(1)} %get-tuple-element.65), channel_id=1, source_target_pairs={{8,0},{16,8},{24,16},{0,24},{9,1},{17,9},{25,17},{1,25},{10,2},{18... | collective-permute-start | bytes 24584 | tf_op jit(solution)/shard_map/ppermute | solution.py:36
  88.6 8.9 %collective-permute-start.25 = (f32[2,132,2]{2,1,0:T(8,128)S(1)}, f32[2,132,2]{2,1,0:T(8,128)S(1)}, u32[]{:S(2)}, u32[]{:S(2)}) collective-permute-start(f32[2,132,2]{2,1,0:T(8,128)S(1)} %get-tuple-element.32), channel_id=1, source_target_pairs={{0,1},{1,2},{2,3},{3,4},{4,5},{5,6},{6,7},{7,0},{8,9},{9,10},{10,1... | collective-permute-start | bytes 6344 | tf_op jit(solution)/shard_map/ppermute | solution.py:34
  88.8 8.7 %collective-permute-start.26 = (f32[2,132,2]{2,1,0:T(8,128)S(1)}, f32[2,132,2]{2,1,0:T(8,128)S(1)}, u32[]{:S(2)}, u32[]{:S(2)}) collective-permute-start(f32[2,132,2]{2,1,0:T(8,128)S(1)} %get-tuple-element.33), channel_id=1, source_target_pairs={{1,0},{2,1},{3,2},{4,3},{5,4},{6,5},{7,6},{0,7},{9,8},{10,9},{11,1... | collective-permute-start | bytes 6344 | tf_op jit(solution)/shard_map/ppermute | solution.py:36
  98.9 3.1 %collective-permute-start.27 = (f32[2,2,512]{2,1,0:T(2,128)S(1)}, f32[2,2,512]{2,1,0:T(2,128)S(1)}, u32[]{:S(2)}, u32[]{:S(2)}) collective-permute-start(f32[2,2,512]{2,1,0:T(2,128)S(1)} %get-tuple-element.60), channel_id=1, source_target_pairs={{0,8},{8,16},{16,24},{24,0},{1,9},{9,17},{17,25},{25,1},{2,10},{10... | collective-permute-start | bytes 24584 | tf_op jit(solution)/shard_map/ppermute | solution.py:34
  99.6 2.5 %collective-permute-start.28 = (f32[2,2,512]{2,1,0:T(2,128)S(1)}, f32[2,2,512]{2,1,0:T(2,128)S(1)}, u32[]{:S(2)}, u32[]{:S(2)}) collective-permute-start(f32[2,2,512]{2,1,0:T(2,128)S(1)} %get-tuple-element.61), channel_id=1, source_target_pairs={{8,0},{16,8},{24,16},{0,24},{9,1},{17,9},{25,17},{1,25},{10,2},{18... | collective-permute-start | bytes 24584 | tf_op jit(solution)/shard_map/ppermute | solution.py:36
  102.2 8.7 %collective-permute-start.29 = (f32[2,132,2]{2,1,0:T(8,128)S(1)}, f32[2,132,2]{2,1,0:T(8,128)S(1)}, u32[]{:S(2)}, u32[]{:S(2)}) collective-permute-start(f32[2,132,2]{2,1,0:T(8,128)S(1)} %get-tuple-element.28), channel_id=1, source_target_pairs={{0,1},{1,2},{2,3},{3,4},{4,5},{5,6},{6,7},{7,0},{8,9},{9,10},{10,1... | collective-permute-start | bytes 6344 | tf_op jit(solution)/shard_map/ppermute | solution.py:34
  102.8 9.0 %collective-permute-start.30 = (f32[2,132,2]{2,1,0:T(8,128)S(1)}, f32[2,132,2]{2,1,0:T(8,128)S(1)}, u32[]{:S(2)}, u32[]{:S(2)}) collective-permute-start(f32[2,132,2]{2,1,0:T(8,128)S(1)} %get-tuple-element.29), channel_id=1, source_target_pairs={{1,0},{2,1},{3,2},{4,3},{5,4},{6,5},{7,6},{0,7},{9,8},{10,9},{11,1... | collective-permute-start | bytes 6344 | tf_op jit(solution)/shard_map/ppermute | solution.py:36
  113.1 3.1 %collective-permute-start.31 = (f32[2,2,512]{2,1,0:T(2,128)S(1)}, f32[2,2,512]{2,1,0:T(2,128)S(1)}, u32[]{:S(2)}, u32[]{:S(2)}) collective-permute-start(f32[2,2,512]{2,1,0:T(2,128)S(1)} %get-tuple-element.56), channel_id=1, source_target_pairs={{0,8},{8,16},{16,24},{24,0},{1,9},{9,17},{17,25},{25,1},{2,10},{10... | collective-permute-start | bytes 24584 | tf_op jit(solution)/shard_map/ppermute | solution.py:34
  113.6 2.7 %collective-permute-start.32 = (f32[2,2,512]{2,1,0:T(2,128)S(1)}, f32[2,2,512]{2,1,0:T(2,128)S(1)}, u32[]{:S(2)}, u32[]{:S(2)}) collective-permute-start(f32[2,2,512]{2,1,0:T(2,128)S(1)} %get-tuple-element.57), channel_id=1, source_target_pairs={{8,0},{16,8},{24,16},{0,24},{9,1},{17,9},{25,17},{1,25},{10,2},{18... | collective-permute-start | bytes 24584 | tf_op jit(solution)/shard_map/ppermute | solution.py:36
  116.5 8.6 %collective-permute-start.33 = (f32[2,132,2]{2,1,0:T(8,128)S(1)}, f32[2,132,2]{2,1,0:T(8,128)S(1)}, u32[]{:S(2)}, u32[]{:S(2)}) collective-permute-start(f32[2,132,2]{2,1,0:T(8,128)S(1)} %get-tuple-element.24), channel_id=1, source_target_pairs={{0,1},{1,2},{2,3},{3,4},{4,5},{5,6},{6,7},{7,0},{8,9},{9,10},{10,1... | collective-permute-start | bytes 6344 | tf_op jit(solution)/shard_map/ppermute | solution.py:34
  116.7 10.5 %collective-permute-start.34 = (f32[2,132,2]{2,1,0:T(8,128)S(1)}, f32[2,132,2]{2,1,0:T(8,128)S(1)}, u32[]{:S(2)}, u32[]{:S(2)}) collective-permute-start(f32[2,132,2]{2,1,0:T(8,128)S(1)} %get-tuple-element.25), channel_id=1, source_target_pairs={{1,0},{2,1},{3,2},{4,3},{5,4},{6,5},{7,6},{0,7},{9,8},{10,9},{11,1... | collective-permute-start | bytes 6344 | tf_op jit(solution)/shard_map/ppermute | solution.py:36
  128.6 3.1 %collective-permute-start.35 = (f32[2,2,512]{2,1,0:T(2,128)S(1)}, f32[2,2,512]{2,1,0:T(2,128)S(1)}, u32[]{:S(2)}, u32[]{:S(2)}) collective-permute-start(f32[2,2,512]{2,1,0:T(2,128)S(1)} %get-tuple-element.52), channel_id=1, source_target_pairs={{0,8},{8,16},{16,24},{24,0},{1,9},{9,17},{17,25},{25,1},{2,10},{10... | collective-permute-start | bytes 24584 | tf_op jit(solution)/shard_map/ppermute | solution.py:34
  128.8 3.0 %collective-permute-start.36 = (f32[2,2,512]{2,1,0:T(2,128)S(1)}, f32[2,2,512]{2,1,0:T(2,128)S(1)}, u32[]{:S(2)}, u32[]{:S(2)}) collective-permute-start(f32[2,2,512]{2,1,0:T(2,128)S(1)} %get-tuple-element.53), channel_id=1, source_target_pairs={{8,0},{16,8},{24,16},{0,24},{9,1},{17,9},{25,17},{1,25},{10,2},{18... | collective-permute-start | bytes 24584 | tf_op jit(solution)/shard_map/ppermute | solution.py:36
  131.9 9.0 %collective-permute-start.37 = (f32[2,132,2]{2,1,0:T(8,128)S(1)}, f32[2,132,2]{2,1,0:T(8,128)S(1)}, u32[]{:S(2)}, u32[]{:S(2)}) collective-permute-start(f32[2,132,2]{2,1,0:T(8,128)S(1)} %get-tuple-element.20), channel_id=1, source_target_pairs={{0,1},{1,2},{2,3},{3,4},{4,5},{5,6},{6,7},{7,0},{8,9},{9,10},{10,1... | collective-permute-start | bytes 6344 | tf_op jit(solution)/shard_map/ppermute | solution.py:34
  132.1 10.2 %collective-permute-start.38 = (f32[2,132,2]{2,1,0:T(8,128)S(1)}, f32[2,132,2]{2,1,0:T(8,128)S(1)}, u32[]{:S(2)}, u32[]{:S(2)}) collective-permute-start(f32[2,132,2]{2,1,0:T(8,128)S(1)} %get-tuple-element.21), channel_id=1, source_target_pairs={{1,0},{2,1},{3,2},{4,3},{5,4},{6,5},{7,6},{0,7},{9,8},{10,9},{11,1... | collective-permute-start | bytes 6344 | tf_op jit(solution)/shard_map/ppermute | solution.py:36
